TPU v7x, 512 devices: a whole 4x4x16 slice. The times are simulated.
512 devices in a mesh: root: 4 (over z_hi, core), col: 128 (over z_lo, y, x).
Axes of the slice: x: 4, y: 4, z: 16 (z_hi: 2, z_lo: 8; z = z_hi * 8 + z_lo), core: 2. Of those that a mesh axis runs over, the one named last changes fastest.
Arguments:
- coeffs: float32 [4, 3072, 3072], P('root', 'col'), may hold values from -6 to 6
- diagonal: float32 [3072, 3072], P('col'), may hold values from -1 to 1
- shift: float32 [4], P('root'), may hold values from -1 to 1
- rotation: float32 [4, 4], replicated, may hold values from -1 to 1, as said below
- string_blocks: bfloat16 [30720, 128], P('col'), may hold values from -0.15625 to 0.15625
- block_cols: int32 [24, 10], replicated, may hold values from 0 to 23, all different within a row
Outputs:
- filtered: float32 [4, 3072, 3072], P('root', 'col')
Inputs may be any that keep to these rules, and one draw needn't show every extreme that they name: `block_cols`: each row names 10 different block columns, and every block column is named by some row. rotation is an orthogonal matrix.
All inputs are finite; a program needn't handle non-finite values.
Results may differ from a plain program's by a relative error of at most 0.0003.
Values may be sent and summed in bfloat16 or wider, within the bound.
A program may use at most 64 MiB of HBM per device.

v0:
```python
import jax
import jax.numpy as jnp
from jax import lax
from jax.sharding import PartitionSpec as P


def apply_blocks(matrix, operator_blocks, block_cols):
    height, breadth = matrix.shape
    nblocks, filled = block_cols.shape
    blocksize = breadth // nblocks
    grouped = matrix.reshape(height, nblocks, blocksize)
    picked = jnp.take(grouped, block_cols, axis=1)
    tiles = operator_blocks.reshape(nblocks, filled, blocksize, blocksize).astype(jnp.float32)
    result = jnp.einsum("rifk,ifjk->rij", picked, tiles, precision=lax.Precision.HIGHEST)
    return result.reshape(height, breadth)


def layout_pieces(stacked):
    count, height, breadth = stacked.shape
    groups = breadth // height
    return (
        stacked.reshape(count, height, groups, height)
        .transpose(0, 2, 1, 3)
        .reshape(count, groups, height * height)
    )


def layout_whole(moved, height):
    count = moved.shape[0]
    groups = moved.shape[1]
    return (
        moved.reshape(count, groups, height, height)
        .transpose(0, 3, 1, 2)
        .reshape(count, height, groups * height)
    )


def swap_layout(stacked):
    moved = lax.all_to_all(layout_pieces(stacked), "col", split_axis=1, concat_axis=1, tiled=True)
    return layout_whole(moved, stacked.shape[1])


def shards(coeffs, diagonal, shift, rotation, string_blocks, block_cols):
    start = coeffs[0]
    energy = shift[0]
    operator_blocks = lax.all_gather(string_blocks, "col", axis=0, tiled=True)

    def apply_local(matrix):
        return apply_blocks(matrix, operator_blocks, block_cols)

    def sigma_local(vector):
        turned = swap_layout(vector[None])[0]
        beta_turned = apply_local(turned)
        beta_part = swap_layout(beta_turned[None])[0]
        return apply_local(vector) + beta_part + diagonal * vector

    first = 0.5 * (sigma_local(start) - energy * start)
    second = sigma_local(first) - energy * first - start
    all_roots = lax.all_gather(second[None], "root", axis=0, tiled=True)
    weights = lax.dynamic_index_in_dim(rotation, lax.axis_index("root"), 0, keepdims=False)
    result = jnp.einsum("s,sba->ba", weights, all_roots, precision=lax.Precision.HIGHEST)
    return result[None]


def solution(mesh):
    return jax.shard_map(
        shards,
        mesh=mesh,
        in_specs=(P("root", "col", None), P("col", None), P("root"), P(), P("col", None), P()),
        out_specs=P("root", "col", None),
        check_vma=False,
    )
```

profile of v0, /device:TPU:1, one launch (start us, length us, event | category | flops | bytes accessed | tf_op | source)
XLA Modules:
  0.0 1165.1 jit_solution(13638159206079844193)
XLA Ops:
  6.5 0.0 copy-start
  6.5 0.0 all-gather.4.cloned.1.call-start
  6.5 0.7 all-gather.4.cloned.1.call-update
  7.3 2.1 reshape_broadcast_in_dim_squeeze.3
  9.4 0.4 copy.61
  9.8 1.0 copy.62
  10.8 20.4 %all-to-all-start = ((f32[1,128,576]{2,0,1:T(1,128)}), f32[1,128,576]{2,0,1:T(1,128)S(1)}, u32[]{:S(2)}, u32[]{:S(2)}) async-start(f32[1,128,576]{2,0,1:T(1,128)} %copy.62), calls=%async_computation | async-start | bytes 655360 | tf_op jit(solution)/shard_map/all_to_all | solution.py:39
  31.2 0.0 copy-done.9
  31.2 0.1 copy.57
  31.3 0.1 reshape.97
  31.4 0.1 copy.55
  31.5 21.5 %all-to-all-done = f32[1,128,576]{2,0,1:T(1,128)S(1)} async-done(((f32[1,128,576]{2,0,1:T(1,128)}), f32[1,128,576]{2,0,1:T(1,128)S(1)}, u32[]{:S(2)}, u32[]{:S(2)}) %all-to-all-start) | async-done | bytes 294944 | tf_op jit(solution)/shard_map/all_to_all | solution.py:39
  52.9 0.2 copy.63
  53.1 0.5 copy.64
  53.6 0.9 reshape_squeeze_reshape.6
  54.6 0.1 copy.66
  54.6 1.0 gather_fusion.1
  55.6 841.9 %all-gather.4.cloned.1.call-done = bf16[30720,128]{1,0:T(8,128)(2,1)} async-done(((bf16[240,128]{1,0:T(8,128)(2,1)}), bf16[30720,128]{1,0:T(8,128)(2,1)}) %all-gather.4.cloned.1.call-update) | async-done | bytes 7864336 | tf_op jit(solution)/shard_map/all_gather | solution.py:46
  897.5 8.5 fusion.25
  906.1 0.0 copy-start.1
  906.1 0.1 copy.67
  906.2 1.0 reshape_broadcast_in_dim_reshape.6
  907.2 0.4 copy.68
  907.6 0.9 copy.69
  908.5 7.4 all-to-all-start.1
  916.0 0.1 copy.96
  916.0 0.1 copy.58
  916.1 1.0 gather_fusion
  917.8 9.2 fusion.22
  927.0 4.3 all-to-all-done.1
  931.3 1.1 copy.70
  932.4 0.5 copy.71
  932.9 0.9 squeeze_reshape.6
  933.8 0.0 copy-done.5
  933.8 0.8 fusion.39
  934.6 0.7 copy-done.2
  935.3 1.1 reshape_broadcast_in_dim.3
  936.5 0.4 copy.76
  936.9 0.2 copy.77
  937.1 27.6 %all_to_all.20 = f32[1,128,576]{2,0,1:T(1,128)S(1)} all-to-all(f32[1,128,576]{2,0,1:T(1,128)S(1)} %copy.77), channel_id=1, replica_groups=mesh['root'=4,'col'=128] {'col'}, dimensions={1} | all-to-all | bytes 589824 | tf_op jit(solution)/shard_map/all_to_all | solution.py:39
  964.7 0.2 copy.78
  964.9 0.5 copy.79
  965.3 0.9 reshape_squeeze_reshape.7
  966.3 0.1 copy.81
  966.3 1.0 gather_fusion.3
  967.4 8.6 fusion.31
  975.9 0.0 copy-start.6
  975.9 0.1 copy.82
  976.0 1.0 reshape_broadcast_in_dim_reshape.7
  977.0 0.4 copy.83
  977.4 0.9 copy.84
  978.4 8.1 all-to-all-start.3
  986.5 0.3 all-gather.6.cloned.1.call-start
  986.9 1.0 gather_fusion.2
  987.9 9.2 fusion.28
  997.1 4.9 all-to-all-done.3
  1002.0 1.1 copy.85
  1003.1 0.5 copy.86
  1003.6 0.9 squeeze_reshape.7
  1004.5 0.8 fusion.36
  1005.3 0.0 all-gather.6.cloned.1.call-update
  1005.3 148.2 %all-gather.6.cloned.1.call-done = f32[96,3072]{1,0:T(8,128)} async-done(((f32[24,3072]{1,0:T(8,128)}), f32[96,3072]{1,0:T(8,128)}) %all-gather.6.cloned.1.call-update) | async-done | bytes 1179664 | tf_op jit(solution)/shard_map/all_gather | solution.py:59
  1153.6 3.9 fusion.20
  1157.5 0.8 copy.92
  (19 shorter events, 0.1 us)
Async XLA Ops:
  6.5 1147.0 %copy-start = (f32[4,4]{1,0:T(4,128)S(1)}, f32[4,4]{1,0:T(4,128)}, u32[]{:S(2)}) copy-start(f32[4,4]{1,0:T(4,128)} %param.11) | copy-start | bytes 196
  6.5 24.6 %copy-start.9 = (s32[24,10]{0,1:T(8,128)S(1)}, s32[24,10]{0,1:T(8,128)}, u32[]{:S(2)}) copy-start(s32[24,10]{0,1:T(8,128)} %param.13) | copy-start | bytes 2884
  6.5 891.0 %all-gather.4.cloned.1.call-start = ((), (), s32[]{:S(2)}) async-start(), calls=%async_computation.4 | async-start | bytes 7925760 | tf_op jit(solution)/shard_map/all_gather | solution.py:46
  10.8 42.2 %all-to-all-start = ((f32[1,128,576]{2,0,1:T(1,128)}), f32[1,128,576]{2,0,1:T(1,128)S(1)}, u32[]{:S(2)}, u32[]{:S(2)}) async-start(f32[1,128,576]{2,0,1:T(1,128)} %copy.62), calls=%async_computation | async-start | bytes 655360 | tf_op jit(solution)/shard_map/all_to_all | solution.py:39
  906.1 9.9 copy-start.1
  908.5 22.7 %all-to-all-start.1 = ((f32[1,128,576]{2,0,1:T(1,128)}), f32[1,128,576]{2,0,1:T(1,128)}, u32[]{:S(2)}, u32[]{:S(2)}) async-start(f32[1,128,576]{2,0,1:T(1,128)} %copy.69), calls=%async_computation.1 | async-start | bytes 655360 | tf_op jit(solution)/shard_map/all_to_all | solution.py:39
  927.0 6.8 copy-start.5
  927.0 6.8 copy-start.7
  934.6 0.7 copy-start.2
  975.9 10.9 copy-start.6
  978.4 23.7 %all-to-all-start.3 = ((f32[1,128,576]{2,0,1:T(1,128)}), f32[1,128,576]{2,0,1:T(1,128)}, u32[]{:S(2)}, u32[]{:S(2)}) async-start(f32[1,128,576]{2,0,1:T(1,128)} %copy.84), calls=%async_computation.3 | async-start | bytes 655360 | tf_op jit(solution)/shard_map/all_to_all | solution.py:39
  986.5 167.0 %all-gather.6.cloned.1.call-start = ((), (), s32[]{:S(2)}) async-start(), calls=%async_computation.5 | async-start | bytes 1474560 | tf_op jit(solution)/shard_map/all_gather | solution.py:59
  997.1 7.4 copy-start.3
  997.1 7.4 copy-start.4
  997.1 7.4 copy-start.8
Sparse Core Ops, SparseCore 0:
  9.4 888.0 all-gather.3
  1005.5 148.0 all-gather.5
where the time goes:
time: 1170 us
  waiting for transfers between devices  1020 us (87%)
  matrix products  39.5 us (3%)
  starting transfers between devices  36.2 us (3%)
  blocking collectives  27.6 us (2%)
  local copies, waits for them, and re-layouts  24.3 us (2%)
  between operations  14.3 us (1%)
    all_gather x1, waiting for transfers between devices, shards(): operator_blocks = lax.all_gather(string_blocks, 'col', axis=0, tiled=True)  842 us
    all_gather x1, waiting for transfers between devices, shards(): all_roots = lax.all_gather(second[None], 'root', axis=0, tiled=True)  148 us
    all_to_all x3, starting transfers between devices, swap_layout(): lax.all_to_all(layout_pieces(stacked), 'col', split_axis=1, concat_axis=1...  35.9 us
    dot_general x4, matrix products, apply_blocks(): jnp.einsum('rifk,ifjk->rij', picked, tiles, precision=lax.Precision.HIGHEST)  35.6 us
    all_to_all x3, waiting for transfers between devices, swap_layout(): lax.all_to_all(layout_pieces(stacked), 'col', split_axis=1, concat_axis=1...  30.6 us
    all_to_all x1, blocking collectives, swap_layout(): lax.all_to_all(layout_pieces(stacked), 'col', split_axis=1, concat_axis=1...  27.6 us
  transfers between devices with their start and end apart: 5, of which 5 were waited for; matrix products, arithmetic and copies ran while one was open for 2% of the time, Pallas kernels for 0%

commit v1 on v0

--- a/solution.py
+++ b/solution.py
@@ -2,6 +2,16 @@
 import jax.numpy as jnp
 from jax import lax
 from jax.sharding import PartitionSpec as P
+
+mark_layers_all_on = lambda group_axis, s0: jnp.concatenate(
+    jax.lax.all_to_all(
+        jnp.stack([s0 for _ in range(jax.lax.psum(1, group_axis))]),
+        group_axis,
+        split_axis=0,
+        concat_axis=0,
+    ),
+    axis=0,
+)
 
 
 def apply_blocks(matrix, operator_blocks, block_cols):
@@ -43,7 +53,7 @@
 def shards(coeffs, diagonal, shift, rotation, string_blocks, block_cols):
     start = coeffs[0]
     energy = shift[0]
-    operator_blocks = lax.all_gather(string_blocks, "col", axis=0, tiled=True)
+    operator_blocks = mark_layers_all_on("col", string_blocks)
 
     def apply_local(matrix):
         return apply_blocks(matrix, operator_blocks, block_cols)

time: 1170 us -> 598 us (0.51)
  waiting for transfers between devices: 1020 us -> 411 us
  blocking collectives: 27.6 us -> 72.1 us
    all_gather x1 -> x0, waiting for transfers between devices: 842 us -> none  [shards(): operator_blocks = lax.all_gather(string_blocks, 'col', axis=0, tiled=True)]
    all_to_all x0 -> x1, waiting for transfers between devices: none -> 339 us  [jax.lax.all_to_all(jnp.stack([s0 for _ in range(jax.lax.psum(1, group_axi...]
    all_gather x1, waiting for transfers between devices: 148 us -> 51.5 us  [shards(): all_roots = lax.all_gather(second[None], 'root', axis=0, tiled=True)]
    all_to_all x1 -> x2, blocking collectives: 27.6 us -> 72.1 us  [swap_layout(): lax.all_to_all(layout_pieces(stacked), 'col', split_axis=1, concat_axis=1...]
    all_to_all x3 -> x2, starting transfers between devices: 35.9 us -> 21.1 us  [swap_layout(): lax.all_to_all(layout_pieces(stacked), 'col', split_axis=1, concat_axis=1...]
    all_to_all x3 -> x2, waiting for transfers between devices: 30.6 us -> 21.1 us  [swap_layout(): lax.all_to_all(layout_pieces(stacked), 'col', split_axis=1, concat_axis=1...]
  transfers between devices with their start and end apart: 5 -> 4, of which waited for: 5 -> 4; matrix products, arithmetic and copies ran while one was open for 2% -> 4% of each run, Pallas kernels for 0% -> 0%
where the time goes in v1:
time: 598 us; the launch traced here: 597 us
  waiting for transfers between devices  411 us (69%)
  blocking collectives  72.1 us (12%)
  matrix products  39.5 us (7%)
  starting transfers between devices  30.6 us (5%)
  local copies, waits for them, and re-layouts  27.8 us (5%)
  between operations  14.3 us (2%)
    all_to_all x1, waiting for transfers between devices, jax.lax.all_to_all(jnp.stack([s0 for _ in range(jax.lax.psum(1, group_axi...  339 us
    all_to_all x2, blocking collectives, swap_layout(): lax.all_to_all(layout_pieces(stacked), 'col', split_axis=1, concat_axis=1...  72.1 us
    all_gather x1, waiting for transfers between devices, shards(): all_roots = lax.all_gather(second[None], 'root', axis=0, tiled=True)  51.5 us
    dot_general x4, matrix products, apply_blocks(): jnp.einsum('rifk,ifjk->rij', picked, tiles, precision=lax.Precision.HIGHEST)  35.6 us
    all_to_all x2, waiting for transfers between devices, swap_layout(): lax.all_to_all(layout_pieces(stacked), 'col', split_axis=1, concat_axis=1...  21.1 us
    all_to_all x2, starting transfers between devices, swap_layout(): lax.all_to_all(layout_pieces(stacked), 'col', split_axis=1, concat_axis=1...  21.1 us
  transfers between devices with their start and end apart: 4, of which 4 were waited for; matrix products, arithmetic and copies ran while one was open for 4% of the time, Pallas kernels for 0%

profile of v1, /device:TPU:1, one launch (start us, length us, event | category | flops | bytes accessed | tf_op | source)
XLA Modules:
  0.0 597.1 jit_solution(15304999667335352467)
XLA Ops:
  6.5 0.0 copy-start
  6.5 2.1 reshape_broadcast_in_dim_squeeze.3
  8.7 0.4 copy.61
  9.1 0.2 copy.62
  9.3 42.0 %all_to_all.25 = f32[1,128,576]{2,0,1:T(1,128)S(1)} all-to-all(f32[1,128,576]{2,0,1:T(1,128)S(1)} %copy.62), channel_id=1, replica_groups=mesh['root'=4,'col'=128] {'col'}, dimensions={1} | all-to-all | bytes 589824 | tf_op jit(solution)/shard_map/all_to_all | solution.py:49
  51.3 4.2 stack.2
  55.5 9.2 %all-to-all-start = ((bf16[128,240,128]{2,1,0:T(8,128)(2,1)}), bf16[128,240,128]{2,1,0:T(8,128)(2,1)}, u32[]{:S(2)}, u32[]{:S(2)}) async-start(bf16[128,240,128]{2,1,0:T(8,128)(2,1)} %stack.2), calls=%async_computation | async-start | bytes 15728640 | tf_op jit(solution)/shard_map/all_to_all | solution.py:7
  64.7 0.0 copy-done.10
  64.7 0.1 copy.57
  64.8 0.1 reshape.92
  64.9 0.1 copy.55
  65.0 0.2 copy.63
  65.2 0.5 copy.64
  65.7 0.9 reshape_squeeze_reshape.6
  66.6 0.1 copy.66
  66.7 1.0 gather_fusion.1
  67.7 338.6 %all-to-all-done = bf16[128,240,128]{2,1,0:T(8,128)(2,1)} async-done(((bf16[128,240,128]{2,1,0:T(8,128)(2,1)}), bf16[128,240,128]{2,1,0:T(8,128)(2,1)}, u32[]{:S(2)}, u32[]{:S(2)}) %all-to-all-start) | async-done | bytes 7864352 | tf_op jit(solution)/shard_map/all_to_all | solution.py:7
  406.3 8.5 %fusion.25 = f32[24,24,128]{2,0,1:T(8,128)S(1)} fusion(bf16[24,10,128,128]{3,2,1,0:T(8,128)(2,1)} %bitcast.4, f32[24,10,24,128]{3,2,1,0:T(8,128)S(1)} %bitcast.122, pred[24,10]{1,0:T(8,128)(4,1)S(1)} %copy.55), kind=kOutput, calls=%fused_computation.27 | convolution fusion | flops 1133199360 | bytes 11108592 | tf_op jit(solution)/shard_map/rifk,ifjk->rij/dot_general | solution.py:24
  414.8 0.0 copy-start.1
  414.9 0.1 copy.67
  414.9 1.0 reshape_broadcast_in_dim_reshape.6
  415.9 0.4 copy.68
  416.4 1.0 copy.69
  417.3 12.0 %all-to-all-start.2 = ((f32[1,128,576]{2,0,1:T(1,128)}), f32[1,128,576]{2,0,1:T(1,128)}, u32[]{:S(2)}, u32[]{:S(2)}) async-start(f32[1,128,576]{2,0,1:T(1,128)} %copy.69), calls=%async_computation.2 | async-start | bytes 655360 | tf_op jit(solution)/shard_map/all_to_all | solution.py:49
  429.3 0.1 copy.96
  429.3 0.1 copy.58
  429.4 1.0 gather_fusion
  431.1 9.2 %fusion.22 = f32[24,3,8,128]{3,2,1,0:T(8,128)} fusion(bf16[24,10,128,128]{3,2,1,0:T(8,128)(2,1)} %bitcast.4, f32[24,10,24,128]{3,2,1,0:T(8,128)S(1)} %bitcast.124, pred[24,10]{1,0:T(8,128)(4,1)S(1)} %copy.55), kind=kOutput, calls=%fused_computation.26 | convolution fusion | flops 1133199360 | bytes 11108592 | tf_op jit(solution)/shard_map/rifk,ifjk->rij/dot_general | solution.py:24
  440.3 10.4 %all-to-all-done.2 = f32[1,128,576]{2,0,1:T(1,128)} async-done(((f32[1,128,576]{2,0,1:T(1,128)}), f32[1,128,576]{2,0,1:T(1,128)}, u32[]{:S(2)}, u32[]{:S(2)}) %all-to-all-start.2) | async-done | bytes 294944 | tf_op jit(solution)/shard_map/all_to_all | solution.py:49
  450.7 1.1 copy.70
  451.8 0.5 copy.71
  452.3 0.9 squeeze_reshape.6
  453.1 0.0 copy-done.7
  453.2 0.8 fusion.39
  453.9 0.7 copy-done.2
  454.7 1.1 reshape_broadcast_in_dim.3
  455.8 0.4 copy.76
  456.3 0.2 copy.77
  456.5 30.1 %all_to_all.26 = f32[1,128,576]{2,0,1:T(1,128)S(1)} all-to-all(f32[1,128,576]{2,0,1:T(1,128)S(1)} %copy.77), channel_id=1, replica_groups=mesh['root'=4,'col'=128] {'col'}, dimensions={1} | all-to-all | bytes 589824 | tf_op jit(solution)/shard_map/all_to_all | solution.py:49
  486.6 0.2 copy.78
  486.8 0.5 copy.79
  487.3 0.9 reshape_squeeze_reshape.7
  488.2 0.1 copy.81
  488.3 1.0 gather_fusion.3
  489.3 8.6 %fusion.31 = f32[24,24,128]{2,0,1:T(8,128)S(1)} fusion(bf16[24,10,128,128]{3,2,1,0:T(8,128)(2,1)} %bitcast.4, f32[24,10,24,128]{3,2,1,0:T(8,128)S(1)} %bitcast.125, pred[24,10]{1,0:T(8,128)(4,1)S(1)} %copy.55), kind=kOutput, calls=%fused_computation.29 | convolution fusion | flops 1133199360 | bytes 11108592 | tf_op jit(solution)/shard_map/rifk,ifjk->rij/dot_general | solution.py:24
  497.8 0.0 copy-start.6
  497.8 0.1 copy.82
  497.9 1.0 reshape_broadcast_in_dim_reshape.7
  498.9 0.4 copy.83
  499.3 1.0 copy.84
  500.3 9.1 %all-to-all-start.4 = ((f32[1,128,576]{2,0,1:T(1,128)}), f32[1,128,576]{2,0,1:T(1,128)}, u32[]{:S(2)}, u32[]{:S(2)}) async-start(f32[1,128,576]{2,0,1:T(1,128)} %copy.84), calls=%async_computation.4 | async-start | bytes 655360 | tf_op jit(solution)/shard_map/all_to_all | solution.py:49
  509.4 0.3 all-gather.3.cloned.1.call-start
  509.7 1.0 gather_fusion.2
  510.8 9.2 %fusion.28 = f32[24,3,8,128]{3,2,1,0:T(8,128)} fusion(bf16[24,10,128,128]{3,2,1,0:T(8,128)(2,1)} %bitcast.4, f32[24,10,24,128]{3,2,1,0:T(8,128)S(1)} %bitcast.123, pred[24,10]{1,0:T(8,128)(4,1)S(1)} %copy.55), kind=kOutput, calls=%fused_computation.28 | convolution fusion | flops 1133199360 | bytes 11108592 | tf_op jit(solution)/shard_map/rifk,ifjk->rij/dot_general | solution.py:24
  520.0 10.7 %all-to-all-done.4 = f32[1,128,576]{2,0,1:T(1,128)} async-done(((f32[1,128,576]{2,0,1:T(1,128)}), f32[1,128,576]{2,0,1:T(1,128)}, u32[]{:S(2)}, u32[]{:S(2)}) %all-to-all-start.4) | async-done | bytes 294944 | tf_op jit(solution)/shard_map/all_to_all | solution.py:49
  530.7 1.1 copy.85
  531.8 0.5 copy.86
  532.3 0.9 squeeze_reshape.7
  533.2 0.8 fusion.36
  534.0 0.0 all-gather.3.cloned.1.call-update
  534.0 51.5 %all-gather.3.cloned.1.call-done = f32[96,3072]{1,0:T(8,128)} async-done(((f32[24,3072]{1,0:T(8,128)}), f32[96,3072]{1,0:T(8,128)}) %all-gather.3.cloned.1.call-update) | async-done | bytes 1179664 | tf_op jit(solution)/shard_map/all_gather | solution.py:69
  585.6 0.0 copy-done
  585.6 3.9 fusion.20
  589.5 0.8 copy.92
  (20 shorter events, 0.1 us)
Async XLA Ops:
  6.5 579.0 %copy-start = (f32[4,4]{1,0:T(4,128)S(1)}, f32[4,4]{1,0:T(4,128)}, u32[]{:S(2)}) copy-start(f32[4,4]{1,0:T(4,128)} %param.11) | copy-start | bytes 196
  6.5 44.8 %copy-start.9 = (bf16[240,128]{1,0:T(8,128)(2,1)S(1)}, bf16[240,128]{1,0:T(8,128)(2,1)}, u32[]{:S(2)}) copy-start(bf16[240,128]{1,0:T(8,128)(2,1)} %param.12) | copy-start | bytes 184324
  55.5 9.2 %copy-start.10 = (s32[24,10]{0,1:T(8,128)S(1)}, s32[24,10]{0,1:T(8,128)}, u32[]{:S(2)}) copy-start(s32[24,10]{0,1:T(8,128)} %param.13) | copy-start | bytes 2884
  55.5 350.8 %all-to-all-start = ((bf16[128,240,128]{2,1,0:T(8,128)(2,1)}), bf16[128,240,128]{2,1,0:T(8,128)(2,1)}, u32[]{:S(2)}, u32[]{:S(2)}) async-start(bf16[128,240,128]{2,1,0:T(8,128)(2,1)} %stack.2), calls=%async_computation | async-start | bytes 15728640 | tf_op jit(solution)/shard_map/all_to_all | solution.py:7
  414.8 14.4 %copy-start.1 = (f32[1,24,3072]{2,1,0:T(8,128)S(1)}, f32[1,24,3072]{2,1,0:T(8,128)}, u32[]{:S(2)}) copy-start(f32[1,24,3072]{2,1,0:T(8,128)} %param.8) | copy-start | bytes 884740
  417.3 33.4 %all-to-all-start.2 = ((f32[1,128,576]{2,0,1:T(1,128)}), f32[1,128,576]{2,0,1:T(1,128)}, u32[]{:S(2)}, u32[]{:S(2)}) async-start(f32[1,128,576]{2,0,1:T(1,128)} %copy.69), calls=%async_computation.2 | async-start | bytes 655360 | tf_op jit(solution)/shard_map/all_to_all | solution.py:49
  440.3 12.8 %copy-start.5 = (f32[24,3,8,128]{3,2,1,0:T(8,128)S(1)}, f32[24,3,8,128]{3,2,1,0:T(8,128)}, u32[]{:S(2)}) copy-start(f32[24,3,8,128]{3,2,1,0:T(8,128)} %fusion.22) | copy-start | bytes 884740
  440.3 12.8 %copy-start.7 = (f32[24,3072]{1,0:T(8,128)S(1)}, f32[24,3072]{1,0:T(8,128)}, u32[]{:S(2)}) copy-start(f32[24,3072]{1,0:T(8,128)} %param.9) | copy-start | bytes 884740
  453.9 0.7 copy-start.2
  497.8 11.9 %copy-start.6 = (f32[3,24,8,128]{3,2,1,0:T(8,128)S(1)}, f32[3,24,8,128]{3,2,1,0:T(8,128)}, u32[]{:S(2)}) copy-start(f32[3,24,8,128]{3,2,1,0:T(8,128)} %get-tuple-element.6) | copy-start | bytes 884740
  500.3 30.4 %all-to-all-start.4 = ((f32[1,128,576]{2,0,1:T(1,128)}), f32[1,128,576]{2,0,1:T(1,128)}, u32[]{:S(2)}, u32[]{:S(2)}) async-start(f32[1,128,576]{2,0,1:T(1,128)} %copy.84), calls=%async_computation.4 | async-start | bytes 655360 | tf_op jit(solution)/shard_map/all_to_all | solution.py:49
  509.4 76.2 %all-gather.3.cloned.1.call-start = ((), (), s32[]{:S(2)}) async-start(), calls=%async_computation.5 | async-start | bytes 1474560 | tf_op jit(solution)/shard_map/all_gather | solution.py:69
  520.0 13.2 %copy-start.3 = (f32[24,3072]{1,0:T(8,128)S(1)}, f32[24,3072]{1,0:T(8,128)}, u32[]{:S(2)}) copy-start(f32[24,3072]{1,0:T(8,128)} %copy-done.2) | copy-start | bytes 884740
  520.0 13.2 %copy-start.4 = (f32[24,3,8,128]{3,2,1,0:T(8,128)S(1)}, f32[24,3,8,128]{3,2,1,0:T(8,128)}, u32[]{:S(2)}) copy-start(f32[24,3,8,128]{3,2,1,0:T(8,128)} %fusion.28) | copy-start | bytes 884740
  520.0 13.2 %copy-start.8 = (f32[24,3072]{1,0:T(8,128)S(1)}, f32[24,3072]{1,0:T(8,128)}, u32[]{:S(2)}) copy-start(f32[24,3072]{1,0:T(8,128)} %param.9) | copy-start | bytes 884740
Sparse Core Ops, SparseCore 0:
  534.2 51.3 all-gather.2
